TPU v7x, 128 devices: a whole 4x4x4 slice. The times are simulated.
128 devices in a mesh: ctx: 32 (over z, x, core), exp: 4 (over y).
Axes of the slice: x: 4, y: 4, z: 4, core: 2. Of those that a mesh axis runs over, the one named last changes fastest.
Arguments:
- queries: bfloat16 [8192, 4096], P('ctx', 'exp'), may hold values from -6 to 6
- key_rows: bfloat16 [8192, 4096], P('ctx', 'exp'), may hold values from -6 to 6
- value_rows: bfloat16 [8192, 4096], P('ctx', 'exp'), may hold values from -6 to 6
- gate_rows: bfloat16 [8192, 4096], P('ctx', 'exp'), may hold values from -6 to 6
- decay_exp: int32 [32], P('exp'), may hold values from 5 to 16
- attn_gain: float32 [4096], P('exp'), may hold values from 0.1 to 1.9
- out_proj: bfloat16 [4096, 6144], P('exp'), may hold values from -0.09375 to 0.09375
- residual: bfloat16 [8192, 6144], P(('ctx', 'exp')), may hold values from -6 to 6
- norm_gain: float32 [6144], replicated, may hold values from 0.1 to 1.9
- routes: int32 [8192, 2], P('ctx'), may hold values from 0 to 31, as said below
- route_weights: float32 [8192, 2], P('ctx'), may hold values from 0.1 to 1
- w_gate: bfloat16 [4, 9216, 6144], P('exp', 'ctx'), may hold values from -0.078125 to 0.078125
- w_up: bfloat16 [4, 9216, 6144], P('exp', 'ctx'), may hold values from -0.078125 to 0.078125
- w_down: bfloat16 [4, 9216, 6144], P('exp', 'ctx'), may hold values from -0.0625 to 0.0625
Outputs:
- layer_out: bfloat16 [8192, 6144], P(('ctx', 'exp'))
Inputs may be any that keep to these rules, and one draw needn't show every extreme that they name: `routes`: A row's two entries differ. An expert e below 4 is named only in column e % 2. In every aligned block of 64 rows each expert below 4 is named at most 8 times, and some expert below 4 exactly 8 times.
All inputs are finite; a program needn't handle non-finite values.
Results may differ from a plain program's by a relative error of at most 0.018.
Values may be sent and summed in bfloat16 or wider, within the bound.
A program may use at most 128 MiB of HBM per device.

v0:
```python
import jax
import jax.numpy as jnp
from jax import lax
from jax.sharding import PartitionSpec as P

EPSILON = 1e-06


def prefix(shard, axis, combine, identity):
    size, index = (lax.axis_size(axis), lax.axis_index(axis))
    everything = jax.tree.map(
        lambda part, kind: lax.all_gather(part.astype(kind), axis),
        shard,
        (jnp.bfloat16, jnp.bfloat16),
    )
    start = jax.tree.map(
        lambda part, zero: jnp.broadcast_to(jnp.asarray(zero, part.dtype), part.shape),
        shard,
        identity,
    )

    def turn(k, before):
        reached = k < index
        new = combine(
            before, jax.tree.map(lambda part, own: part[k].astype(own.dtype), everything, shard)
        )
        return jax.tree.map(lambda a, b: jnp.where(reached, a, b), new, before)

    return lax.fori_loop(0, size, turn, start)


def span_local(queries, key_rows, value_rows, decay_exp):
    row_count = queries.shape[0]
    head_count = decay_exp.shape[0]
    head_width = queries.shape[1] // head_count
    query_heads = queries.reshape(row_count, head_count, head_width)
    key_heads = key_rows.reshape(row_count, head_count, head_width)
    value_heads = value_rows.reshape(row_count, head_count, head_width)
    decay_rates = jnp.exp2(-decay_exp.astype(jnp.float32))
    positions = jnp.arange(row_count, dtype=jnp.float32)
    offsets = positions[:, None] - positions[None, :]
    damping = jnp.where(
        offsets[None] >= 0.0,
        jnp.exp(-decay_rates[:, None, None] * jnp.maximum(offsets, 0.0)[None]),
        0.0,
    )
    scores = jnp.einsum("thd,shd->hts", query_heads, key_heads, preferred_element_type=jnp.float32)
    mixing = (scores * damping).astype(jnp.bfloat16)
    inner_part = jnp.einsum("hts,shd->thd", mixing, value_heads, preferred_element_type=jnp.float32)
    tail_decay = jnp.exp(-decay_rates[None, :] * (row_count - 1.0 - positions)[:, None])
    keyed_rows = (key_heads.astype(jnp.float32) * tail_decay[:, :, None]).astype(jnp.bfloat16)
    update = jnp.einsum("shd,she->hde", keyed_rows, value_heads, preferred_element_type=jnp.float32)
    carry_decay = jnp.exp(-decay_rates * row_count)
    lead_decay = jnp.exp(-decay_rates[None, :] * (positions + 1.0)[:, None])
    leading = query_heads.astype(jnp.float32) * lead_decay[:, :, None]
    return (inner_part, leading, update, carry_decay)


def join_states(earlier, later):
    return (earlier[0] * later[0], later[0][:, None, None] * earlier[1] + later[1])


def settle(inner_part, leading, prior_state, gate_rows, attn_gain):
    outer_part = jnp.einsum("thd,hde->the", leading, prior_state, precision=lax.Precision.HIGHEST)
    mixed_heads = inner_part + outer_part
    row_count, head_count, head_width = mixed_heads.shape
    mean_square = jnp.mean(mixed_heads * mixed_heads, axis=2, keepdims=True)
    normed_heads = mixed_heads * lax.rsqrt(mean_square + EPSILON)
    gain_heads = attn_gain.reshape(head_count, head_width)
    gate_heads = gate_rows.reshape(row_count, head_count, head_width).astype(jnp.float32)
    settled = (normed_heads * gain_heads * jax.nn.sigmoid(gate_heads)).astype(jnp.bfloat16)
    return settled.reshape(row_count, head_count * head_width)


def token_norm(hidden, norm_gain):
    mean_square = jnp.mean(hidden * hidden, axis=1, keepdims=True)
    return (hidden * lax.rsqrt(mean_square + EPSILON) * norm_gain).astype(jnp.bfloat16)


def slot_tables(owners, chosen_ids, weights, capacity):
    column = owners % 2
    chosen = jnp.where(column[:, None] == 0, chosen_ids[None, :, 0], chosen_ids[None, :, 1])
    weight_rows = jnp.where(column[:, None] == 0, weights[None, :, 0], weights[None, :, 1])
    picked = chosen == owners[:, None]
    slot_rank = jnp.cumsum(picked.astype(jnp.int32), axis=1) - 1
    slot_ids = jnp.arange(capacity, dtype=jnp.int32)
    slot_table = picked[:, None, :] & (slot_rank[:, None, :] == slot_ids[None, :, None])
    return (slot_table.astype(jnp.bfloat16), jnp.where(slot_table, weight_rows[:, None, :], 0.0))


def expert_part(slot_rows, gate_cols, up_cols, down_rows):
    contract_dims = (((1,), (1,)), ((), ()))
    first_half = lax.dot_general(
        slot_rows, gate_cols, contract_dims, preferred_element_type=jnp.float32
    )
    second_half = lax.dot_general(
        slot_rows, up_cols, contract_dims, preferred_element_type=jnp.float32
    )
    activated = (jax.nn.silu(first_half) * second_half).astype(jnp.bfloat16)
    return jnp.dot(activated, down_rows, preferred_element_type=jnp.float32)


def body(
    queries,
    key_rows,
    value_rows,
    gate_rows,
    decay_exp,
    attn_gain,
    out_proj,
    residual,
    norm_gain,
    routes,
    route_weights,
    w_gate,
    w_up,
    w_down,
):
    inner_part, leading, update, carry_decay = span_local(queries, key_rows, value_rows, decay_exp)
    head_count = decay_exp.shape[0]
    head_width = queries.shape[1] // head_count
    identity = (
        jnp.ones((head_count,), jnp.float32),
        jnp.zeros((head_count, head_width, head_width), jnp.float32),
    )
    carried, prior_state = prefix((carry_decay, update), "ctx", join_states, identity)
    settled = settle(inner_part, leading, prior_state, gate_rows, attn_gain)
    span_rows = queries.shape[0]
    group_count = lax.axis_size("exp")
    group_rows = span_rows // group_count
    group_index = lax.axis_index("exp")
    first_mine = group_index * group_rows
    capacity = group_rows // 8
    gate_cols = w_gate[0]
    up_cols = w_up[0]
    down_rows = w_down[0]
    placed = lax.dynamic_update_slice_in_dim(
        jnp.zeros((span_rows, residual.shape[1]), jnp.float32),
        residual.astype(jnp.float32),
        first_mine,
        0,
    )
    projected = jnp.dot(settled, out_proj, preferred_element_type=jnp.float32) + placed
    hidden_all = lax.psum(projected.astype(jnp.bfloat16), "exp").astype(jnp.float32)
    normed_all = token_norm(hidden_all, norm_gain)
    owners = jnp.reshape(group_index, (1,))
    slot_table, weighted = slot_tables(owners, routes, route_weights, capacity * group_count)
    outgoing = jnp.einsum(
        "ecn,nd->cd", slot_table, normed_all, preferred_element_type=jnp.float32
    ).astype(jnp.bfloat16)
    gathered = lax.all_gather(outgoing, "ctx", axis=0, tiled=True)
    produced = lax.psum_scatter(
        expert_part(gathered, gate_cols, up_cols, down_rows).astype(jnp.bfloat16),
        "ctx",
        scatter_dimension=0,
        tiled=True,
    ).astype(jnp.float32)
    spread_back = jnp.einsum("ecn,cd->nd", weighted, produced, precision=lax.Precision.HIGHEST)
    mixture = lax.psum_scatter(
        spread_back.astype(jnp.bfloat16), "exp", scatter_dimension=0, tiled=True
    ).astype(jnp.float32)
    hidden = lax.dynamic_slice_in_dim(hidden_all, first_mine, group_rows, 0)
    return (hidden + mixture).astype(jnp.bfloat16)


def solution(mesh):
    in_specs = (
        P("ctx", "exp"),
        P("ctx", "exp"),
        P("ctx", "exp"),
        P("ctx", "exp"),
        P("exp"),
        P("exp"),
        P("exp", None),
        P(("ctx", "exp"), None),
        P(),
        P("ctx", None),
        P("ctx", None),
        P("exp", "ctx", None),
        P("exp", "ctx", None),
        P("exp", "ctx", None),
    )
    out_specs = P(("ctx", "exp"), None)
    return jax.shard_map(body, mesh=mesh, in_specs=in_specs, out_specs=out_specs, check_vma=False)
```

profile of v0, /device:TPU:1, one launch (start us, length us, event | category | flops | bytes accessed | tf_op | source)
XLA Modules:
  0.0 523.0 jit_solution(2067149946234657723)
XLA Ops:
  7.9 2.1 copy.36
  10.7 2.2 convolution_convert_fusion.3
  15.6 65.4 %all-reduce = bf16[256]{0:T(256)(128)(2,1)S(1)} all-reduce(bf16[256]{0:T(256)(128)(2,1)S(1)} %dynamic-update-slice.1), channel_id=2, replica_groups=mesh['ctx'=32,'exp'=4] {'ctx'}, use_global_device_ids=true, to_apply=%add | all-reduce | flops 256 | bytes 1024
  81.7 2.3 add_divide_fusion
  84.0 2.6 copy.34
  88.1 86.4 %while.14 = (s32[]{:T(128)}, f32[8,128,128]{2,1,0:T(8,128)}, s32[]{:T(128)}, bf16[32,8]{1,0:T(8,128)(2,1)}, bf16[32,8,128,128]{3,2,1,0:T(8,128)(2,1)}, /*index=5*/s32[]{:T(128)}, s32[]{:T(128)}) while((s32[]{:T(128)}, f32[8,128,128]{2,1,0:T(8,128)}, s32[]{:T(128)}, bf16[32,8]{1,0:T(8,128)(2,1)}, ...), condition=%wide.region_1.2_spmd.clone, body=%wide.region_0.1_spmd.clone.sunk | while | flops 655372 | bytes 1310905 | solution.py:29
  91.3 2.0 fusion.70
  94.1 2.0 fusion.70
  96.8 2.0 fusion.70
  99.5 2.0 fusion.70
  102.2 2.0 fusion.70
  104.9 2.0 fusion.70
  107.7 2.0 fusion.70
  110.3 2.0 fusion.70
  113.0 2.0 fusion.70
  115.6 2.0 fusion.70
  118.3 2.0 fusion.70
  120.9 2.0 fusion.70
  123.6 2.0 fusion.70
  126.3 2.0 fusion.70
  128.9 2.0 fusion.70
  131.7 2.0 fusion.70
  134.4 2.0 fusion.70
  137.1 2.0 fusion.70
  139.8 2.0 fusion.70
  142.5 2.0 fusion.70
  145.3 2.0 fusion.70
  148.0 2.0 fusion.70
  150.7 2.0 fusion.70
  153.4 2.0 fusion.70
  156.2 2.0 fusion.70
  158.9 2.0 fusion.70
  161.6 2.0 fusion.70
  174.5 3.6 convolution_bitcast_fusion
  178.1 3.7 multiply_reduce_fusion.1
  183.6 6.7 %fusion.57 = f32[256,6144]{1,0:T(8,128)S(1)} fusion(bf16[256,1024]{0,1:T(8,128)(2,1)S(1)} %bitcast.89, bf16[1024,6144]{1,0:T(8,128)(2,1)} %param.22), kind=kOutput, calls=%fused_computation.78 | convolution fusion | flops 3221225472 | bytes 19398656 | tf_op jit(solution)/shard_map/dot_general | solution.py:143
  190.6 2.1 convert_element_type.110
  193.5 76.0 %all-reduce.3.cloned.1.call-done = bf16[256,6144]{1,0:T(8,128)(2,1)} async-done(((bf16[256,6144]{1,0:T(8,128)(2,1)}), bf16[256,6144]{1,0:T(8,128)(2,1)}) %all-reduce.3.cloned.1.call-update) | async-done | bytes 3145744 | tf_op jit(solution)/shard_map/psum | solution.py:144
  269.6 2.6 multiply_reduce_fusion
  272.2 3.7 convolution_convert_fusion.2
  276.1 63.1 %all-gather.5.cloned.1.call-done = bf16[1024,6144]{1,0:T(8,128)(2,1)} async-done(((bf16[32,6144]{1,0:T(8,128)(2,1)}), bf16[1024,6144]{1,0:T(8,128)(2,1)}) %all-gather.5.cloned.1.call-update) | async-done | bytes 12582928 | tf_op jit(solution)/shard_map/all_gather | solution.py:151
  339.2 10.5 %fusion.4 = f32[1024,288]{0,1:T(8,128)} fusion(bf16[1024,6144]{1,0:T(8,128)(2,1)} %all-gather.5.cloned.1.call-done, bf16[1,288,6144]{2,1,0:T(8,128)(2,1)} %param.27), kind=kOutput, calls=%fused_computation.11 | convolution fusion | flops 3623878656 | bytes 17301504 | tf_op jit(solution)/shard_map/dot_general | solution.py:93
  349.7 17.7 %convolution_convert_fusion = bf16[1024,6144]{1,0:T(8,128)(2,1)} fusion(bf16[1,288,6144]{2,1,0:T(8,128)(2,1)S(1)} %copy-done, bf16[1024,6144]{1,0:T(8,128)(2,1)} %all-gather.5.cloned.1.call-done, bf16[1,288,6144]{2,1,0:T(8,128)(2,1)} %param.28, f32[1024,288]{0,1:T(8,128)} %fusion.4), kind=kOutput, calls=%fused_computation.3 | convolution fusion | flops 7255818240 | bytes 33423360 | tf_op jit(solution)/shard_map/dot_general | solution.py:100
  368.0 101.9 %reduce-scatter.3.cloned.1.call-done = bf16[32,6144]{1,0:T(8,128)(2,1)} async-done(((bf16[1024,6144]{1,0:T(8,128)(2,1)}), bf16[32,6144]{1,0:T(8,128)(2,1)}) %reduce-scatter.3.cloned.1.call-update) | async-done | bytes 393232 | tf_op jit(solution)/shard_map/reduce_scatter | solution.py:152
  469.9 5.1 convolution_convert_fusion.1
  475.1 5.4 %convert_element_type.111 = f32[256,6144]{1,0:T(8,128)} convert(bf16[256,6144]{1,0:T(8,128)(2,1)} %all-reduce.3.cloned.1.call-done) | non-fusion elementwise | flops 1572864 | bytes 9437184 | tf_op jit(solution)/shard_map/convert_element_type | solution.py:144
  480.5 33.3 %reduce-scatter.5.cloned.1.call-done = bf16[64,6144]{1,0:T(8,128)(2,1)} async-done(((bf16[256,6144]{1,0:T(8,128)(2,1)}), bf16[64,6144]{1,0:T(8,128)(2,1)}) %reduce-scatter.5.cloned.1.call-update) | async-done | bytes 786448 | tf_op jit(solution)/shard_map/reduce_scatter | solution.py:159
  513.8 2.7 add_convert_fusion
  (85 shorter events, 41.5 us)
Async XLA Ops:
  6.5 343.1 %copy-start = (bf16[1,288,6144]{2,1,0:T(8,128)(2,1)S(1)}, bf16[1,288,6144]{2,1,0:T(8,128)(2,1)}, u32[]{:S(2)}) copy-start(bf16[1,288,6144]{2,1,0:T(8,128)(2,1)} %param.29) | copy-start | bytes 10616836
  6.5 81.6 %all-gather.7.cloned.1.call-start = ((), (), s32[]{:S(2)}) async-start(), calls=%async_computation.6 | async-start | bytes 8650752 | tf_op jit(solution)/shard_map/all_gather | solution.py:12
  12.9 256.7 %all-reduce.3.cloned.1.call-start = ((), (), s32[]{:S(2)}) async-start(), calls=%async_computation.2 | async-start | bytes 6291456 | tf_op jit(solution)/shard_map/psum | solution.py:144
  88.1 90.0 %copy-start.6 = (f32[8]{0:T(128)S(1)}, f32[8]{0:T(128)}, u32[]{:S(2)}) copy-start(f32[8]{0:T(128)} %get-tuple-element.131) | copy-start | bytes 100
  174.5 7.3 %copy-start.3 = (f32[1024]{0:T(1024)S(1)}, f32[1024]{0:T(1024)}, u32[]{:S(2)}) copy-start(f32[1024]{0:T(1024)} %param.21) | copy-start | bytes 12292
  183.6 6.7 %copy-start.2 = (bf16[64,6144]{1,0:T(8,128)(2,1)S(1)}, bf16[64,6144]{1,0:T(8,128)(2,1)}, u32[]{:S(2)}) copy-start(bf16[64,6144]{1,0:T(8,128)(2,1)} %param.23) | copy-start | bytes 2359300
  190.6 2.2 copy-start.5
  192.7 146.5 %all-gather.5.cloned.1.call-start = ((), (), s32[]{:S(2)}) async-start(), calls=%async_computation.3 | async-start | bytes 12976128 | tf_op jit(solution)/shard_map/all_gather | solution.py:151
  275.9 194.0 %reduce-scatter.3.cloned.1.call-start = ((), (), s32[]{:S(2)}) async-start(), calls=%async_computation.4 | async-start | bytes 12976128 | tf_op jit(solution)/shard_map/reduce_scatter | solution.py:152
  367.3 0.7 copy-start.4
  367.4 146.5 %reduce-scatter.5.cloned.1.call-start = ((), (), s32[]{:S(2)}) async-start(), calls=%async_computation.5 | async-start | bytes 3932160 | tf_op jit(solution)/shard_map/reduce_scatter | solution.py:159
  475.0 41.5 %copy-start.1 = (bf16[1,288,6144]{2,1,0:T(8,128)(2,1)S(1)}, bf16[1,288,6144]{2,1,0:T(8,128)(2,1)}, u32[]{:S(2)}) copy-start(bf16[1,288,6144]{2,1,0:T(8,128)(2,1)} %param.29) | copy-start | bytes 10616836
Sparse Core Ops, SparseCore 0:
  13.0 56.8 all-gather.6
  192.8 76.7 all-reduce.2
  276.0 63.1 all-gather.4
  367.5 102.3 reduce-scatter.2
  475.2 38.6 reduce-scatter.4
where the time goes:
time: 525 us; the launch traced here: 523 us
  waiting for transfers between devices  274 us (52%)
  other arithmetic  108 us (21%)
  blocking collectives  65.4 us (12%)
  matrix products  53 us (10%)
  between operations  13.8 us (3%)
  local copies, waits for them, and re-layouts  8.36 us (2%)
    reduce_scatter x1, waiting for transfers between devices, body(): lax.psum_scatter(expert_part(gathered, gate_cols, up_cols, down_rows).ast...  102 us
    psum x1, waiting for transfers between devices, body(): lax.psum(projected.astype(jnp.bfloat16), 'exp').astype(jnp.float32)  76 us
    unnamed x1, blocking collectives  65.4 us
    select_n x32, other arithmetic, turn(): return jax.tree.map(lambda a, b: jnp.where(reached, a, b), new, before)  65.1 us
    all_gather x1, waiting for transfers between devices, body(): gathered = lax.all_gather(outgoing, 'ctx', axis=0, tiled=True)  63.1 us
    reduce_scatter x1, waiting for transfers between devices, body(): lax.psum_scatter(spread_back.astype(jnp.bfloat16), 'exp', scatter_dimensi...  33.3 us
    convert_element_type x32, other arithmetic, turn(): part[k].astype(own.dtype)  21.3 us
    dot_general x1, matrix products, expert_part(): return jnp.dot(activated, down_rows, preferred_element_type=jnp.float32)  17.7 us
  transfers between devices with their start and end apart: 5, of which 4 were waited for; matrix products, arithmetic and copies ran while one was open for 3% of the time, Pallas kernels for 0%

commit v1 on v0

--- a/solution.py
+++ b/solution.py
@@ -148,7 +148,9 @@
     outgoing = jnp.einsum(
         "ecn,nd->cd", slot_table, normed_all, preferred_element_type=jnp.float32
     ).astype(jnp.bfloat16)
-    gathered = lax.all_gather(outgoing, "ctx", axis=0, tiled=True)
+    gathered = jnp.concatenate(
+        lax.all_to_all(jnp.stack([outgoing] * lax.axis_size("ctx")), "ctx", 0, 0), axis=0
+    )
     produced = lax.psum_scatter(
         expert_part(gathered, gate_cols, up_cols, down_rows).astype(jnp.bfloat16),
         "ctx",

time: 525 us -> 614 us (1.17)
  blocking collectives: 65.4 us -> 214 us
  waiting for transfers between devices: 274 us -> 211 us
  local copies, waits for them, and re-layouts: 8.36 us -> 19 us
  matrix products: 53 us -> 46.7 us
    all_to_all x0 -> x1, blocking collectives: none -> 149 us  [body(): lax.all_to_all(jnp.stack([outgoing] * lax.axis_size('ctx')), 'ctx', 0, 0)]
    all_gather x1 -> x0, waiting for transfers between devices: 63.1 us -> none  [body(): gathered = lax.all_gather(outgoing, 'ctx', axis=0, tiled=True)]
    another operation x2 -> x3, local copies, waits for them, and re-layouts: 0.08 us -> 6.22 us  [the longest x1 6.14 us: body(): jnp.stack([outgoing] * lax.axis_size('ctx'))]
  transfers between devices with their start and end apart: 5 -> 4, of which waited for: 4 -> 3; matrix products, arithmetic and copies ran while one was open for 3% -> 2% of each run, Pallas kernels for 0% -> 0%
where the time goes in v1:
time: 614 us; the launch traced here: 612 us
  blocking collectives  214 us (35%)
  waiting for transfers between devices  211 us (34%)
  other arithmetic  107 us (17%)
  matrix products  46.7 us (8%)
  local copies, waits for them, and re-layouts  19 us (3%)
  between operations  13.8 us (2%)
    all_to_all x1, blocking collectives, body(): lax.all_to_all(jnp.stack([outgoing] * lax.axis_size('ctx')), 'ctx', 0, 0)  149 us
    reduce_scatter x1, waiting for transfers between devices, body(): lax.psum_scatter(expert_part(gathered, gate_cols, up_cols, down_rows).ast...  101 us
    psum x1, waiting for transfers between devices, body(): lax.psum(projected.astype(jnp.bfloat16), 'exp').astype(jnp.float32)  76 us
    unnamed x1, blocking collectives  65.4 us
    select_n x32, other arithmetic, turn(): return jax.tree.map(lambda a, b: jnp.where(reached, a, b), new, before)  65.1 us
    reduce_scatter x1, waiting for transfers between devices, body(): lax.psum_scatter(spread_back.astype(jnp.bfloat16), 'exp', scatter_dimensi...  33.5 us
    convert_element_type x32, other arithmetic, turn(): part[k].astype(own.dtype)  21.3 us
    dot_general x1, matrix products, expert_part(): return jnp.dot(activated, down_rows, preferred_element_type=jnp.float32)  17.6 us
  transfers between devices with their start and end apart: 4, of which 3 were waited for; matrix products, arithmetic and copies ran while one was open for 2% of the time, Pallas kernels for 0%

profile of v1, /device:TPU:1, one launch (start us, length us, event | category | flops | bytes accessed | tf_op | source)
XLA Modules:
  0.0 611.9 jit_solution(1556892502988688035)
XLA Ops:
  7.9 2.1 copy.36
  10.7 2.2 convolution_convert_fusion.3
  15.6 65.4 %all-reduce = bf16[256]{0:T(256)(128)(2,1)S(1)} all-reduce(bf16[256]{0:T(256)(128)(2,1)S(1)} %dynamic-update-slice.1), channel_id=2, replica_groups=mesh['ctx'=32,'exp'=4] {'ctx'}, use_global_device_ids=true, to_apply=%add | all-reduce | flops 256 | bytes 1024
  81.7 2.3 add_divide_fusion
  84.0 2.6 copy.34
  88.1 86.4 %while.14 = (s32[]{:T(128)}, f32[8,128,128]{2,1,0:T(8,128)}, s32[]{:T(128)}, bf16[32,8]{1,0:T(8,128)(2,1)}, bf16[32,8,128,128]{3,2,1,0:T(8,128)(2,1)}, /*index=5*/s32[]{:T(128)}, s32[]{:T(128)}) while((s32[]{:T(128)}, f32[8,128,128]{2,1,0:T(8,128)}, s32[]{:T(128)}, bf16[32,8]{1,0:T(8,128)(2,1)}, ...), condition=%wide.region_1.2_spmd.clone, body=%wide.region_0.1_spmd.clone.sunk | while | flops 655372 | bytes 1310905 | solution.py:29
  91.3 2.0 fusion.70
  94.1 2.0 fusion.70
  96.8 2.0 fusion.70
  99.5 2.0 fusion.70
  102.2 2.0 fusion.70
  104.9 2.0 fusion.70
  107.7 2.0 fusion.70
  110.3 2.0 fusion.70
  113.0 2.0 fusion.70
  115.6 2.0 fusion.70
  118.3 2.0 fusion.70
  120.9 2.0 fusion.70
  123.6 2.0 fusion.70
  126.3 2.0 fusion.70
  128.9 2.0 fusion.70
  131.7 2.0 fusion.70
  134.4 2.0 fusion.70
  137.1 2.0 fusion.70
  139.8 2.0 fusion.70
  142.5 2.0 fusion.70
  145.3 2.0 fusion.70
  148.0 2.0 fusion.70
  150.7 2.0 fusion.70
  153.4 2.0 fusion.70
  156.2 2.0 fusion.70
  174.5 3.6 convolution_bitcast_fusion
  178.1 3.7 multiply_reduce_fusion.1
  183.6 6.7 %fusion.57 = f32[256,6144]{1,0:T(8,128)S(1)} fusion(bf16[256,1024]{0,1:T(8,128)(2,1)S(1)} %bitcast.92, bf16[1024,6144]{1,0:T(8,128)(2,1)} %param.22), kind=kOutput, calls=%fused_computation.78 | convolution fusion | flops 3221225472 | bytes 19398656 | tf_op jit(solution)/shard_map/dot_general | solution.py:143
  190.6 2.1 convert_element_type.110
  193.5 76.0 %all-reduce.3.cloned.1.call-done = bf16[256,6144]{1,0:T(8,128)(2,1)} async-done(((bf16[256,6144]{1,0:T(8,128)(2,1)}), bf16[256,6144]{1,0:T(8,128)(2,1)}) %all-reduce.3.cloned.1.call-update) | async-done | bytes 3145744 | tf_op jit(solution)/shard_map/psum | solution.py:144
  269.6 2.6 multiply_reduce_fusion
  272.2 2.9 convolution_convert_fusion.2
  275.1 6.1 %stack.2 = bf16[32,32,6144]{2,1,0:T(8,128)(2,1)} broadcast(bf16[32,6144]{1,0:T(8,128)(2,1)S(1)} %convolution_convert_fusion.2), dimensions={1,2} | broadcast | bytes 12976128 | tf_op jit(solution)/shard_map/stack | solution.py:152
  281.2 148.7 %all_to_all.5 = bf16[32,32,6144]{2,1,0:T(8,128)(2,1)S(1)} all-to-all(bf16[32,32,6144]{2,1,0:T(8,128)(2,1)} %stack.2), channel_id=1, replica_groups=mesh['ctx'=32,'exp'=4] {'ctx'}, dimensions={0} | all-to-all | bytes 25165824 | tf_op jit(solution)/shard_map/all_to_all | solution.py:152
  429.9 4.5 copy-done.1
  434.4 4.9 fusion.4
  439.3 17.6 %convolution_convert_fusion = bf16[1024,6144]{1,0:T(8,128)(2,1)} fusion(bf16[1,288,6144]{2,1,0:T(8,128)(2,1)S(1)} %copy-done, bf16[1024,6144]{1,0:T(8,128)(2,1)} %bitcast.90, bf16[1,288,6144]{2,1,0:T(8,128)(2,1)} %param.28, f32[1024,288]{0,1:T(8,128)} %fusion.4), kind=kOutput, calls=%fused_computation.3 | convolution fusion | flops 7255818240 | bytes 33423360 | tf_op jit(solution)/shard_map/dot_general | solution.py:100
  457.7 101.1 %reduce-scatter.3.cloned.1.call-done = bf16[32,6144]{1,0:T(8,128)(2,1)} async-done(((bf16[1024,6144]{1,0:T(8,128)(2,1)}), bf16[32,6144]{1,0:T(8,128)(2,1)}) %reduce-scatter.3.cloned.1.call-update) | async-done | bytes 393232 | tf_op jit(solution)/shard_map/reduce_scatter | solution.py:154
  558.8 5.1 convolution_convert_fusion.1
  563.9 5.3 convert_element_type.111
  569.2 33.5 %reduce-scatter.5.cloned.1.call-done = bf16[64,6144]{1,0:T(8,128)(2,1)} async-done(((bf16[256,6144]{1,0:T(8,128)(2,1)}), bf16[64,6144]{1,0:T(8,128)(2,1)}) %reduce-scatter.5.cloned.1.call-update) | async-done | bytes 786448 | tf_op jit(solution)/shard_map/reduce_scatter | solution.py:161
  602.7 2.7 add_convert_fusion
  (86 shorter events, 45.4 us)
Async XLA Ops:
  6.5 432.8 %copy-start = (bf16[1,288,6144]{2,1,0:T(8,128)(2,1)S(1)}, bf16[1,288,6144]{2,1,0:T(8,128)(2,1)}, u32[]{:S(2)}) copy-start(bf16[1,288,6144]{2,1,0:T(8,128)(2,1)} %param.29) | copy-start | bytes 10616836
  6.5 81.6 %all-gather.4.cloned.1.call-start = ((), (), s32[]{:S(2)}) async-start(), calls=%async_computation.6 | async-start | bytes 8650752 | tf_op jit(solution)/shard_map/all_gather | solution.py:12
  12.9 256.7 %all-reduce.3.cloned.1.call-start = ((), (), s32[]{:S(2)}) async-start(), calls=%async_computation.3 | async-start | bytes 6291456 | tf_op jit(solution)/shard_map/psum | solution.py:144
  88.1 90.0 %copy-start.6 = (f32[8]{0:T(128)S(1)}, f32[8]{0:T(128)}, u32[]{:S(2)}) copy-start(f32[8]{0:T(128)} %get-tuple-element.131) | copy-start | bytes 100
  174.5 7.3 %copy-start.3 = (f32[1024]{0:T(1024)S(1)}, f32[1024]{0:T(1024)}, u32[]{:S(2)}) copy-start(f32[1024]{0:T(1024)} %param.21) | copy-start | bytes 12292
  183.6 6.7 %copy-start.2 = (bf16[64,6144]{1,0:T(8,128)(2,1)S(1)}, bf16[64,6144]{1,0:T(8,128)(2,1)}, u32[]{:S(2)}) copy-start(bf16[64,6144]{1,0:T(8,128)(2,1)} %param.23) | copy-start | bytes 2359300
  190.6 2.2 copy-start.5
  192.7 366.1 %reduce-scatter.3.cloned.1.call-start = ((), (), s32[]{:S(2)}) async-start(), calls=%async_computation.4 | async-start | bytes 12976128 | tf_op jit(solution)/shard_map/reduce_scatter | solution.py:154
  281.2 153.2 %copy-start.7 = (bf16[1,288,6144]{2,1,0:T(8,128)(2,1)S(1)}, bf16[1,288,6144]{2,1,0:T(8,128)(2,1)}, u32[]{:S(2)}) copy-start(bf16[1,288,6144]{2,1,0:T(8,128)(2,1)} %param.27) | copy-start | bytes 10616836
  429.9 4.5 copy-start.1
  457.0 0.7 copy-start.4
  457.0 145.7 %reduce-scatter.5.cloned.1.call-start = ((), (), s32[]{:S(2)}) async-start(), calls=%async_computation.5 | async-start | bytes 3932160 | tf_op jit(solution)/shard_map/reduce_scatter | solution.py:161
Sparse Core Ops, SparseCore 0:
  13.0 56.8 all-gather.3
  192.8 76.7 all-reduce.2
  457.1 101.5 reduce-scatter.2
  564.0 38.5 reduce-scatter.4
